TPU v7x, 256 devices: a whole 4x4x8 slice. The times are simulated.
256 devices in a mesh: req: 32 (over x, z_lo, core), tp: 8 (over y, z_hi).
Axes of the slice: x: 4, y: 4, z: 8 (z_hi: 2, z_lo: 4; z = z_hi * 4 + z_lo), core: 2. Of those that a mesh axis runs over, the one named last changes fastest.
Arguments:
- queries: bfloat16 [4096, 4096], P('req', 'tp'), may hold values from -12 to 12
- keys_values: bfloat16 [4096, 1024], P('req', 'tp'), may hold values from -12 to 12
- segments: int32 [4096], P('req'), may hold values from 0 to 2, as said below
- sink_logits: float32 [64], P('tp'), may hold values from 0 to 4
- out_weight: bfloat16 [4096, 2880], P('tp'), may hold values from -0.09375 to 0.09375
- out_bias: bfloat16 [2880], replicated, may hold values from -3 to 3
- residual: bfloat16 [4096, 2880], P(('req', 'tp')), may hold values from -6 to 6
- norm_gain: bfloat16 [2880], replicated, may hold values from 0.5 to 1.5
- route_ids: int32 [4096, 4], P(('req', 'tp')), may hold values from 0 to 31, all different within a row; in each aligned block of 16 rows (0 to 15, 16 to 31, ...) at most 4 rows name the same one
- route_logits: float32 [4096, 4], P(('req', 'tp')), may hold values from -6 to 6
- gate_weight: bfloat16 [32, 2880, 2880], P('req', None, 'tp'), may hold values from -0.3125 to 0.3125
- gate_bias: bfloat16 [32, 2880], P('req', 'tp'), may hold values from -3 to 3
- up_weight: bfloat16 [32, 2880, 2880], P('req', None, 'tp'), may hold values from -0.3125 to 0.3125
- up_bias: bfloat16 [32, 2880], P('req', 'tp'), may hold values from -3 to 3
- down_weight: bfloat16 [32, 2880, 2880], P('req', 'tp'), may hold values from -0.0546875 to 0.0546875
- down_bias: bfloat16 [32, 2880], replicated, may hold values from -3 to 3
- page_table: int32 [32, 8], P('req'), may hold values from 0 to 7, each once within a row
Outputs:
- mixed_out: bfloat16 [4096, 2880], P(('req', 'tp'))
- kv_cache: bfloat16 [256, 16, 1024], P('req', None, 'tp')
Inputs may be any that keep to these rules, and one draw needn't show every extreme that they name: `segments`: within each group of 128 tokens the numbers start at 0, never fall and rise by at most one from token to token; every group holds exactly 3 packed requests, of uneven lengths. `route_ids`: each row names 4 different experts. Among the 16 rows of one device no expert is named by more than 4 rows, a bound that some block reaches. `page_table`: each row names every page of its group once.
All inputs are finite; a program needn't handle non-finite values.
Results may differ from a plain program's by a relative error of at most 0.018.
Values may be sent and summed in bfloat16 or wider, within the bound.
A program may use at most 64 MiB of HBM per device.

v0:
```python
import jax
import jax.numpy as jnp
from jax import lax
from jax.sharding import PartitionSpec as P

HEAD = 64
PAGE_LEN = 16


rope_base = 150000.0
norm_eps = 1e-05
swiglu_limit = 7.0
glu_alpha = 1.702


def seg_positions(segment_ids):
    length = segment_ids.shape[0]
    indices = jnp.arange(length, dtype=jnp.int32)
    change = jnp.concatenate([jnp.ones((1,), dtype=bool), segment_ids[1:] != segment_ids[:-1]])
    starts = lax.cummax(jnp.where(change, indices, 0), axis=0)
    return indices - starts


def rotate(values, positions):
    half_dim = values.shape[-1] // 2
    inverse = rope_base ** (-jnp.arange(half_dim, dtype=jnp.float32) / half_dim)
    angles = positions.astype(jnp.float32)[:, None] * inverse[None, :]
    cosine = jnp.cos(angles)[:, None, :]
    sine_col = jnp.sin(angles)[:, None, :]
    first_half = values[..., :half_dim]
    second_half = values[..., half_dim:]
    return jnp.concatenate(
        [
            first_half * cosine - second_half * sine_col,
            second_half * cosine + first_half * sine_col,
        ],
        axis=-1,
    )


def attend_group(queries, keys_values, segment_ids, sink_logits):
    length = queries.shape[0]
    kv_heads = keys_values.shape[1] // (2 * HEAD)
    q_heads = queries.shape[1] // HEAD
    group_size = q_heads // kv_heads
    positions = seg_positions(segment_ids)
    q_rot = rotate(queries.astype(jnp.float32).reshape(length, q_heads, HEAD), positions).astype(
        jnp.bfloat16
    )
    q_rot = q_rot.reshape(length, kv_heads, group_size, HEAD)
    key_part = keys_values.reshape(length, kv_heads, 2, HEAD)
    k_rot = rotate(key_part[:, :, 0].astype(jnp.float32), positions).astype(jnp.bfloat16)
    values = key_part[:, :, 1]
    scores = jnp.einsum(
        "qkgd,skd->kgqs", q_rot, k_rot, preferred_element_type=jnp.float32
    ) * HEAD ** (-0.5)
    indices = jnp.arange(length, dtype=jnp.int32)
    visible = (segment_ids[:, None] == segment_ids[None, :]) & (
        indices[None, :] <= indices[:, None]
    )
    scores = jnp.where(visible, scores, -jnp.inf)
    sink_col = sink_logits.reshape(kv_heads, group_size)[:, :, None]
    highest = jnp.maximum(jnp.max(scores, axis=-1), sink_col)
    expo_terms = jnp.exp(scores - highest[..., None])
    denominator = jnp.sum(expo_terms, axis=-1) + jnp.exp(sink_col - highest)
    probabilities = (expo_terms / denominator[..., None]).astype(jnp.bfloat16)
    attended = jnp.einsum(
        "kgqs,skd->qkgd", probabilities, values, preferred_element_type=jnp.float32
    )
    attended = attended.astype(jnp.bfloat16).reshape(length, q_heads * HEAD)
    cached = jnp.stack([k_rot, values], axis=2).reshape(length, kv_heads * 2 * HEAD)
    return (attended, cached)


def slot_index(routes, experts, capacity):
    blocks, row_count, route_width = routes.shape
    flat_ids = routes.reshape(blocks, row_count * route_width)
    onehot = (flat_ids[:, :, None] == jnp.arange(experts, dtype=jnp.int32)[None, None, :]).astype(
        jnp.int32
    )
    earlier = jnp.cumsum(onehot, axis=1) - onehot
    position = jnp.sum(earlier * onehot, axis=2)
    block_ids = jnp.arange(blocks, dtype=jnp.int32)[:, None]
    slot_ids = flat_ids * (blocks * capacity) + block_ids * capacity + position
    return slot_ids.reshape(blocks * row_count, route_width).astype(jnp.int32)


def dispatch(tokens, slot_ids, slot_total):
    row_count = tokens.shape[0]
    owners = jnp.broadcast_to(jnp.arange(row_count, dtype=jnp.int32)[:, None], slot_ids.shape)
    member = (
        jnp.full((slot_total,), row_count, jnp.int32)
        .at[slot_ids.reshape(-1)]
        .set(owners.reshape(-1))
    )
    padded = jnp.concatenate([tokens, jnp.zeros((1, tokens.shape[1]), tokens.dtype)], axis=0)
    return padded[member]


def body(
    queries,
    keys_values,
    segments,
    sink_logits,
    out_weight,
    out_bias,
    residual,
    norm_gain,
    route_ids,
    route_logits,
    gate_weight,
    gate_bias,
    up_weight,
    up_bias,
    down_weight,
    down_bias,
    page_table,
):
    attended, cached = attend_group(queries, keys_values, segments, sink_logits)
    projected = lax.psum_scatter(
        jnp.dot(attended, out_weight, preferred_element_type=jnp.float32).astype(jnp.bfloat16),
        "tp",
        scatter_dimension=0,
        tiled=True,
    ).astype(jnp.float32)
    hidden = (residual.astype(jnp.float32) + projected + out_bias.astype(jnp.float32)).astype(
        jnp.bfloat16
    )
    stream = hidden.astype(jnp.float32)
    normed = (
        stream
        * lax.rsqrt(jnp.mean(stream * stream, axis=-1, keepdims=True) + norm_eps)
        * norm_gain.astype(jnp.float32)
    ).astype(jnp.bfloat16)
    route_weights = jax.nn.softmax(route_logits, axis=-1)
    tok_count, route_width = route_ids.shape
    experts = down_bias.shape[0]
    model_width = residual.shape[1]
    capacity = max(2, 2 * tok_count * route_width // experts)
    own_slots = slot_index(route_ids[None], experts, capacity)
    group_rows, group_routes = (
        lax.all_gather(normed, "tp", axis=0, tiled=True),
        lax.all_gather(route_ids, "tp", axis=0, tiled=True),
    )
    tp_count = group_rows.shape[0] // tok_count
    all_slots = slot_index(
        group_routes.reshape(tp_count, tok_count, route_width), experts, capacity
    )
    dispatched = dispatch(group_rows, all_slots, experts * tp_count * capacity).reshape(
        experts, tp_count, capacity, model_width
    )
    received = lax.all_to_all(dispatched, "req", split_axis=0, concat_axis=0, tiled=True)
    slot_shape = received.shape
    flat_rows = received.reshape(-1, model_width)
    gate_act = jnp.dot(flat_rows, gate_weight[0], preferred_element_type=jnp.float32) + gate_bias[
        0
    ].astype(jnp.float32)
    up_act = jnp.dot(flat_rows, up_weight[0], preferred_element_type=jnp.float32) + up_bias[
        0
    ].astype(jnp.float32)
    gate_act = jnp.minimum(gate_act, swiglu_limit)
    up_act = jnp.clip(up_act, -swiglu_limit, swiglu_limit)
    active = (gate_act * jax.nn.sigmoid(glu_alpha * gate_act) * (up_act + 1.0)).astype(jnp.bfloat16)
    partial_value = jnp.dot(active, down_weight[0], preferred_element_type=jnp.float32).reshape(
        slot_shape
    )
    summed = lax.psum_scatter(
        partial_value.astype(jnp.bfloat16), "tp", scatter_dimension=1, tiled=True
    ).astype(jnp.float32)
    returned = lax.all_to_all(
        summed.astype(jnp.bfloat16), "req", split_axis=0, concat_axis=0, tiled=True
    ).astype(summed.dtype)
    returned = returned.reshape(experts * capacity, model_width)
    slot_onehot = (
        own_slots[:, :, None] == jnp.arange(experts * capacity, dtype=jnp.int32)[None, None, :]
    ).astype(jnp.float32)
    combiner = jnp.einsum("rk,rks->rs", route_weights, slot_onehot, precision=lax.Precision.HIGHEST)
    expert_onehot = (
        route_ids[:, :, None] == jnp.arange(experts, dtype=jnp.int32)[None, None, :]
    ).astype(jnp.float32)
    dense_weights = jnp.einsum(
        "rk,rke->re", route_weights, expert_onehot, precision=lax.Precision.HIGHEST
    )
    expert_mix = jnp.dot(
        combiner, returned, precision=lax.Precision.HIGHEST, preferred_element_type=jnp.float32
    )
    expert_mix = expert_mix + jnp.dot(
        dense_weights,
        down_bias.astype(jnp.float32),
        precision=lax.Precision.HIGHEST,
        preferred_element_type=jnp.float32,
    )
    mixed_out = (stream + expert_mix).astype(jnp.bfloat16)
    blocks = cached.reshape(-1, PAGE_LEN, cached.shape[1])
    page_pool = jnp.zeros_like(blocks).at[page_table[0]].set(blocks)
    return (mixed_out, page_pool)


def solution(mesh):
    in_specs = (
        P("req", "tp"),
        P("req", "tp"),
        P("req"),
        P("tp"),
        P("tp", None),
        P(),
        P(("req", "tp"), None),
        P(),
        P(("req", "tp"), None),
        P(("req", "tp"), None),
        P("req", None, "tp"),
        P("req", "tp"),
        P("req", None, "tp"),
        P("req", "tp"),
        P("req", "tp", None),
        P(),
        P("req", None),
    )
    out_specs = (P(("req", "tp"), None), P("req", None, "tp"))
    return jax.shard_map(body, mesh=mesh, in_specs=in_specs, out_specs=out_specs, check_vma=False)
```

profile of v0, /device:TPU:1, one launch (start us, length us, event | category | flops | bytes accessed | tf_op | source)
XLA Modules:
  0.0 542.4 jit_solution(17542637364020571878)
XLA Ops:
  7.3 0.9 compare_bitcast_fusion
  8.2 0.8 fusion.23
  9.0 0.1 copy.56
  9.2 0.2 reduce-window.8
  9.3 0.1 reduce.3
  9.5 1.0 copy.57
  10.5 0.9 copy.55
  11.3 0.1 multiply_cosine_fusion
  11.5 0.1 fusion.32
  11.7 0.3 fusion.49
  12.0 0.7 broadcast_maximum_fusion
  12.9 0.2 convolution_convert_fusion.2
  13.2 2.0 convolution_convert_fusion.1
  15.2 37.4 %all-gather = s32[8,16,4]{1,2,0:T(4,128)S(1)} all-gather(s32[1,16,4]{1,2,0:T(4,128)S(1)} %bitcast.89), channel_id=1, replica_groups=mesh['req'=32,'tp'=8] {'tp'}, dimensions={0}, use_global_device_ids=true | all-gather | bytes 2304 | tf_op jit(solution)/shard_map/all_gather | solution.py:143
  52.8 0.1 copy.62
  52.9 0.1 mul.193
  53.0 1.4 fusion.50
  54.7 0.1 reshape.551
  54.8 2.4 scatter_custom_fusion
  57.3 40.8 %reduce-scatter.3.cloned.1.call-done = bf16[16,2880]{1,0:T(8,128)(2,1)} async-done(((bf16[128,2880]{1,0:T(8,128)(2,1)}), bf16[16,2880]{1,0:T(8,128)(2,1)}) %reduce-scatter.3.cloned.1.call-update) | async-done | bytes 92176 | tf_op jit(solution)/shard_map/reduce_scatter | solution.py:120
  98.1 1.0 fusion.16
  99.3 46.0 %all_gather.6 = bf16[128,2880]{1,0:T(8,128)(2,1)S(1)} all-gather(bf16[16,2880]{1,0:T(8,128)(2,1)S(1)} %fusion.18), channel_id=1, replica_groups=mesh['req'=32,'tp'=8] {'tp'}, dimensions={0}, use_global_device_ids=true | all-gather | bytes 829440 | tf_op jit(solution)/shard_map/all_gather | solution.py:142
  145.3 1.0 concatenate.52
  146.3 12.9 %gather_fusion = bf16[1024,2880]{1,0:T(8,128)(2,1)} fusion(bf16[129,2880]{1,0:T(8,128)(2,1)} %concatenate.52, s32[1024]{0:T(1024)S(1)} %fusion.41), kind=kCustom, calls=%fused_computation | custom fusion | bytes 11800576 | tf_op jit(solution)/shard_map/gather | solution.py:97
  159.2 10.7 %reshape.531 = bf16[32,8,4,2880]{3,2,1,0:T(4,128)(2,1)} reshape(bf16[1024,2880]{1,0:T(8,128)(2,1)} %gather_fusion) | data formatting | bytes 11796480 | tf_op jit(solution)/shard_map/reshape | solution.py:149
  169.9 14.4 %all-to-all-start = ((bf16[32,8,4,2880]{3,2,1,0:T(4,128)(2,1)}), bf16[32,8,4,2880]{3,2,1,0:T(4,128)(2,1)}, u32[]{:S(2)}, u32[]{:S(2)}) async-start(bf16[32,8,4,2880]{3,2,1,0:T(4,128)(2,1)} %reshape.531), calls=%async_computation.1 | async-start | bytes 12058624 | tf_op jit(solution)/shard_map/all_to_all | solution.py:152
  184.3 0.2 reduce-scatter.5.cloned.1.call-start
  184.6 133.6 %all-to-all-done = bf16[32,8,4,2880]{3,2,1,0:T(4,128)(2,1)} async-done(((bf16[32,8,4,2880]{3,2,1,0:T(4,128)(2,1)}), bf16[32,8,4,2880]{3,2,1,0:T(4,128)(2,1)}, u32[]{:S(2)}, u32[]{:S(2)}) %all-to-all-start) | async-done | bytes 5898272 | tf_op jit(solution)/shard_map/all_to_all | solution.py:152
  318.2 10.2 %reshape.532 = bf16[1024,2880]{1,0:T(8,128)(2,1)} reshape(bf16[32,8,4,2880]{3,2,1,0:T(4,128)(2,1)} %all-to-all-done) | data formatting | bytes 11796480 | tf_op jit(solution)/shard_map/reshape | solution.py:154
  328.4 6.0 %fusion.3 = f32[1024,360]{0,1:T(8,128)S(1)} fusion(bf16[1024,2880]{1,0:T(8,128)(2,1)} %reshape.532, bf16[1,2880,360]{1,2,0:T(8,128)(2,1)} %param.29), kind=kOutput, calls=%fused_computation.9 | convolution fusion | flops 2123366400 | bytes 9446400 | tf_op jit(solution)/shard_map/dot_general | solution.py:158
  334.4 3.8 multiply_convert_fusion
  338.3 2.3 copy.65
  340.5 2.4 dot_general.38
  342.9 5.2 convolution_convert_fusion
  348.1 4.4 copy.67
  352.8 0.1 reduce_window_sum.22
  352.9 147.3 %reduce-scatter.5.cloned.1.call-done = bf16[32,1,4,2880]{3,0,2,1:T(8,128)(2,1)} async-done(((bf16[32,8,4,2880]{3,0,2,1:T(8,128)(2,1)}), bf16[32,1,4,2880]{3,0,2,1:T(8,128)(2,1)}) %reduce-scatter.5.cloned.1.call-update) | async-done | bytes 737296 | tf_op jit(solution)/shard_map/reduce_scatter | solution.py:167
  500.1 2.4 copy.68
  502.5 6.6 %all-to-all-start.1 = ((bf16[32,1,4,2880]{3,2,1,0:T(4,128)(2,1)}), bf16[32,1,4,2880]{3,2,1,0:T(4,128)(2,1)}, u32[]{:S(2)}, u32[]{:S(2)}) async-start(bf16[32,1,4,2880]{3,2,1,0:T(4,128)(2,1)} %copy.68), calls=%async_computation.3 | async-start | bytes 1507328 | tf_op jit(solution)/shard_map/all_to_all | solution.py:170
  509.1 0.2 select_reduce_fusion
  509.6 0.1 copy.70
  509.8 0.7 scatter_fusion
  510.6 0.3 fusion.26
  510.8 0.3 fusion.25
  511.1 19.7 %all-to-all-done.1 = bf16[32,1,4,2880]{3,2,1,0:T(4,128)(2,1)} async-done(((bf16[32,1,4,2880]{3,2,1,0:T(4,128)(2,1)}), bf16[32,1,4,2880]{3,2,1,0:T(4,128)(2,1)}, u32[]{:S(2)}, u32[]{:S(2)}) %all-to-all-start.1) | async-done | bytes 737312 | tf_op jit(solution)/shard_map/all_to_all | solution.py:170
  530.8 2.3 reshape.533
  533.1 1.5 fusion.51
  534.7 0.9 fusion.1
  (66 shorter events, 1.6 us)
Async XLA Ops:
  7.2 5.9 %copy-start = (bf16[512,2880]{0,1:T(8,128)(2,1)S(1)}, bf16[512,2880]{0,1:T(8,128)(2,1)}, u32[]{:S(2)}) copy-start(bf16[512,2880]{0,1:T(8,128)(2,1)} %param.21) | copy-start | bytes 8847364
  7.2 5.6 %copy-start.9 = (f32[8]{0:T(128)S(1)}, f32[8]{0:T(128)}, u32[]{:S(2)}) copy-start(f32[8]{0:T(128)} %param.20) | copy-start | bytes 100
  7.2 90.9 %reduce-scatter.3.cloned.1.call-start = ((), (), s32[]{:S(2)}) async-start(), calls=%async_computation.4 | async-start | bytes 847872 | tf_op jit(solution)/shard_map/reduce_scatter | solution.py:120
  13.1 2.1 copy-start.7
  13.1 2.1 copy-start.8
  13.1 2.1 copy-start.6
  13.2 85.0 %copy-start.4 = (bf16[16,2880]{1,0:T(8,128)(2,1)S(1)}, bf16[16,2880]{1,0:T(8,128)(2,1)}, u32[]{:S(2)}) copy-start(bf16[16,2880]{1,0:T(8,128)(2,1)} %param.23) | copy-start | bytes 276484
  169.9 14.7 %copy-start.10 = (bf16[1,360]{1,0:T(2,128)(2,1)S(1)}, bf16[1,360]{1,0:T(2,128)(2,1)}, u32[]{:S(2)}) copy-start(bf16[1,360]{1,0:T(2,128)(2,1)} %param.30) | copy-start | bytes 2164
  169.9 14.7 %copy-start.11 = (bf16[1,360]{1,0:T(2,128)(2,1)S(1)}, bf16[1,360]{1,0:T(2,128)(2,1)}, u32[]{:S(2)}) copy-start(bf16[1,360]{1,0:T(2,128)(2,1)} %param.28) | copy-start | bytes 2164
  169.9 148.3 %all-to-all-start = ((bf16[32,8,4,2880]{3,2,1,0:T(4,128)(2,1)}), bf16[32,8,4,2880]{3,2,1,0:T(4,128)(2,1)}, u32[]{:S(2)}, u32[]{:S(2)}) async-start(bf16[32,8,4,2880]{3,2,1,0:T(4,128)(2,1)} %reshape.531), calls=%async_computation.1 | async-start | bytes 12058624 | tf_op jit(solution)/shard_map/all_to_all | solution.py:152
  184.3 315.9 %reduce-scatter.5.cloned.1.call-start = ((), (), s32[]{:S(2)}) async-start(), calls=%async_computation.5 | async-start | bytes 6782976 | tf_op jit(solution)/shard_map/reduce_scatter | solution.py:167
  328.4 6.0 %copy-start.1 = (bf16[1024,2880]{1,0:T(8,128)(2,1)S(1)}, bf16[1024,2880]{1,0:T(8,128)(2,1)}, u32[]{:S(2)}) copy-start(bf16[1024,2880]{1,0:T(8,128)(2,1)} %reshape.532) | copy-start | bytes 17694724
  328.4 6.0 %copy-start.12 = (bf16[1,2880,360]{1,2,0:T(8,128)(2,1)S(1)}, bf16[1,2880,360]{1,2,0:T(8,128)(2,1)}, u32[]{:S(2)}) copy-start(bf16[1,2880,360]{1,2,0:T(8,128)(2,1)} %param.27) | copy-start | bytes 6220804
  352.5 156.9 %copy-start.5 = (f32[16,4]{0,1:T(4,128)S(1)}, f32[16,4]{0,1:T(4,128)}, u32[]{:S(2)}) copy-start(f32[16,4]{0,1:T(4,128)} %param.26) | copy-start | bytes 772
  352.5 157.3 %copy-start.13 = (s32[1,8]{1,0:T(1,128)S(1)}, s32[1,8]{1,0:T(1,128)}, u32[]{:S(2)}) copy-start(s32[1,8]{1,0:T(1,128)} %param.33) | copy-start | bytes 100
  502.5 32.1 %copy-start.2 = (bf16[32,2880]{1,0:T(8,128)(2,1)S(1)}, bf16[32,2880]{1,0:T(8,128)(2,1)}, u32[]{:S(2)}) copy-start(bf16[32,2880]{1,0:T(8,128)(2,1)} %param.32) | copy-start | bytes 552964
  502.5 28.3 %all-to-all-start.1 = ((bf16[32,1,4,2880]{3,2,1,0:T(4,128)(2,1)}), bf16[32,1,4,2880]{3,2,1,0:T(4,128)(2,1)}, u32[]{:S(2)}, u32[]{:S(2)}) async-start(bf16[32,1,4,2880]{3,2,1,0:T(4,128)(2,1)} %copy.68), calls=%async_computation.3 | async-start | bytes 1507328 | tf_op jit(solution)/shard_map/all_to_all | solution.py:170
  510.6 25.0 %copy-start.3 = (bf16[8,16,128]{2,1,0:T(8,128)(2,1)}, bf16[8,16,128]{2,1,0:T(8,128)(2,1)S(1)}, u32[]{:S(2)}) copy-start(bf16[8,16,128]{2,1,0:T(8,128)(2,1)S(1)} %scatter_fusion) | copy-start | bytes 98308
Sparse Core Ops, SparseCore 0:
  15.3 82.7 reduce-scatter.2
  352.6 147.4 reduce-scatter.4
where the time goes:
time: 544 us; the launch traced here: 542 us
  waiting for transfers between devices  341 us (63%)
  blocking collectives  83.5 us (15%)
  local copies, waits for them, and re-layouts  55 us (10%)
  starting transfers between devices  21.3 us (4%)
  matrix products  20.4 us (4%)
  between operations  14.5 us (3%)
  other arithmetic  6.3 us (1%)
    reduce_scatter x1, waiting for transfers between devices, body(): lax.psum_scatter(partial_value.astype(jnp.bfloat16), 'tp', scatter_dimens...  147 us
    all_to_all x1, waiting for transfers between devices, body(): lax.all_to_all(dispatched, 'req', split_axis=0, concat_axis=0, tiled=True)  134 us
    all_gather x1, blocking collectives, body(): lax.all_gather(normed, 'tp', axis=0, tiled=True)  46 us
    reduce_scatter x1, waiting for transfers between devices, body(): lax.psum_scatter(jnp.dot(attended, out_weight, preferred_element_type=jnp...  40.8 us
    all_gather x1, blocking collectives, body(): lax.all_gather(route_ids, 'tp', axis=0, tiled=True)  37.4 us
    all_to_all x1, waiting for transfers between devices, body(): lax.all_to_all(summed.astype(jnp.bfloat16), 'req', split_axis=0, concat_a...  19.7 us
    all_to_all x1, starting transfers between devices, body(): lax.all_to_all(dispatched, 'req', split_axis=0, concat_axis=0, tiled=True)  14.4 us
    gather x1, local copies, waits for them, and re-layouts, dispatch(): return padded[member]  12.9 us
  transfers between devices with their start and end apart: 4, of which 4 were waited for; matrix products, arithmetic and copies ran while one was open for 1% of the time, Pallas kernels for 0%

commit v1 on v0

v1 whole, which is shorter than its diff:
```python
import functools

import jax
import jax.numpy as jnp
from jax import lax
from jax.experimental import pallas as pl
from jax.experimental.pallas import tpu as pltpu
from jax.sharding import PartitionSpec as P

HEAD = 64
PAGE_LEN = 16
MESH = pl.DeviceIdType.MESH

rope_base = 150000.0
norm_eps = 1e-05
swiglu_limit = 7.0
glu_alpha = 1.702

X, Y, Z, C = 4, 4, 8, 2
META = 64
F32, BF16 = jnp.float32, jnp.bfloat16


def coords():
    r, t = lax.axis_index("req"), lax.axis_index("tp")
    return r // 8, t // 2, (t % 2) * 4 + (r // 2) % 4, r % 2


def device(x, y, z, c):
    return (x * 8 + (z % 4) * 2 + c, y * 2 + z // 4)


def entry_barrier(peers):
    barrier = pltpu.get_barrier_semaphore()
    for peer in peers:
        pl.semaphore_signal(barrier, inc=1, device_id=peer, device_id_type=MESH)
    pl.semaphore_wait(barrier, len(peers))


def remote(src, dst, send, recv, peer):
    return pltpu.make_async_remote_copy(
        src_ref=src, dst_ref=dst, send_sem=send, recv_sem=recv, device_id=peer, device_id_type=MESH
    )


def vmem(count):
    return [pl.BlockSpec(memory_space=pltpu.VMEM)] * count


def project_kernel(
    part, residual, bias, gain, meta, toks, hidden, from_y, from_z, stage,
    y_send, y_recv, p_send, p_recv, z_send, z_recv, c_send, c_recv,
):
    x, y, z, c = coords()
    zh = z // 4
    width = part.shape[1]
    y_peer = [device(x, (y + d) % Y, z, c) for d in range(Y)]
    z_peer = [device(x, y, (z + d) % Z, c) for d in range(Z)]
    partner = device(x, y, z, 1 - c)
    entry_barrier(y_peer[1:] + z_peer[1:] + [partner])
    sends = []
    for d in (2, 1, 3):
        rows = pl.ds(pl.multiple_of(((y + d) % Y) * 32, 32), 32)
        copy = remote(part.at[rows], from_y.at[d - 1], y_send.at[d - 1], y_recv.at[d - 1], y_peer[d])
        copy.start()
        sends.append(copy)
    for copy in sends:
        copy.wait_recv()

    def summed(half):
        at = pl.multiple_of(half * 16, 16)
        total = part[pl.ds(pl.multiple_of(y * 32 + half * 16, 16), 16), :].astype(F32)
        for d in range(Y - 1):
            total = total + from_y[d, pl.ds(at, 16), :].astype(F32)
        return total

    stage[...] = summed(1 - zh).astype(BF16)
    swap = remote(stage, from_z, p_send, p_recv, z_peer[4])
    swap.start()
    own = summed(zh) + residual[...].astype(F32) + bias[...].astype(F32)
    swap.wait_recv()
    rounded = (own + from_z[...].astype(F32)).astype(BF16)
    hidden[...] = rounded
    stream = rounded.astype(F32)
    scale = lax.rsqrt(jnp.mean(stream * stream, axis=-1, keepdims=True) + norm_eps)
    slot = c * Z + z
    toks[slot, :, 0:width] = (stream * scale * gain[...].astype(F32)).astype(BF16)
    toks[slot, :, width : width + META] = meta[...]
    z_copies = {}
    for d in (4, 3, 5, 2, 6, 1, 7):
        copy = remote(toks.at[slot], toks.at[slot], z_send.at[d - 1], z_recv.at[d - 1], z_peer[d])
        copy.start()
        z_copies[d] = copy
    crossings = []
    for d in (0, 1, 7, 2, 6, 3, 5, 4):
        if d:
            z_copies[d].wait_recv()
        block = c * Z + (z - d + Z) % Z
        copy = remote(toks.at[block], toks.at[block], c_send.at[d], c_recv.at[d], partner)
        copy.start()
        crossings.append(copy)
    for copy in crossings:
        copy.wait_recv()
    for copy in sends + [swap] + list(z_copies.values()) + crossings:
        copy.wait_send()


def project(part, residual, bias, gain, meta):
    width = part.shape[1]
    rows = residual.shape[0]
    return pl.pallas_call(
        project_kernel,
        out_shape=(
            jax.ShapeDtypeStruct((C * Z, rows, width + META), BF16),
            jax.ShapeDtypeStruct((rows, width), BF16),
        ),
        in_specs=vmem(5),
        out_specs=tuple(vmem(2)),
        scratch_shapes=[
            pltpu.VMEM((Y - 1, 2 * rows, width), BF16),
            pltpu.VMEM((rows, width), BF16),
            pltpu.VMEM((rows, width), BF16),
            pltpu.SemaphoreType.DMA((Y - 1,)),
            pltpu.SemaphoreType.DMA((Y - 1,)),
            pltpu.SemaphoreType.DMA,
            pltpu.SemaphoreType.DMA,
            pltpu.SemaphoreType.DMA((Z - 1,)),
            pltpu.SemaphoreType.DMA((Z - 1,)),
            pltpu.SemaphoreType.DMA((Z,)),
            pltpu.SemaphoreType.DMA((Z,)),
        ],
        compiler_params=pltpu.CompilerParams(collective_id=0, has_side_effects=True),
        name="project_gather",
    )(part, residual, bias, gain, meta)


def spread_kernel(chosen, out, x_send, x_recv, local, n_send, n_recv, f_send, f_recv):
    x, y, z, c = coords()
    x_peer = [device((x + d) % X, y, z, c) for d in range(X)]
    right, left = device(x, (y + 1) % Y, z, c), device(x, (y + Y - 1) % Y, z, c)
    entry_barrier(x_peer[1:] + [right, left])
    here = pltpu.make_async_copy(chosen.at[x], out.at[y, x], local)
    here.start()
    x_copies = {}
    for d in (2, 1, 3):
        copy = remote(
            chosen.at[(x + d) % X], out.at[y, x], x_send.at[d - 1], x_recv.at[d - 1], x_peer[d]
        )
        copy.start()
        x_copies[d] = copy
    order = (0, 1, 3, 2)
    copies = {}
    for d in order:
        if d:
            x_copies[d].wait_recv()
        else:
            here.wait()
        block = out.at[y, (x - d + X) % X]
        for way, peer in ((0, right), (1, left)):
            copies[way, d] = remote(block, block, n_send.at[way, d], n_recv.at[way, d], peer)
            copies[way, d].start()
    relays = []
    for d in order:
        for way, peer, origin in ((0, right, (y + Y - 1) % Y), (1, left, (y + 1) % Y)):
            copies[way, d].wait_recv()
            if d % 2 == way:
                block = out.at[origin, (x - d + X) % X]
                copy = remote(block, block, f_send.at[way, d // 2], f_recv.at[way, d // 2], peer)
                copy.start()
                relays.append(copy)
    for copy in relays:
        copy.wait_recv()
    for copy in list(x_copies.values()) + list(copies.values()) + relays:
        copy.wait_send()


def spread(chosen):
    _, rows, width = chosen.shape
    return pl.pallas_call(
        spread_kernel,
        out_shape=jax.ShapeDtypeStruct((Y, X, rows, width), BF16),
        in_specs=vmem(1),
        out_specs=vmem(1)[0],
        scratch_shapes=[
            pltpu.SemaphoreType.DMA((X - 1,)),
            pltpu.SemaphoreType.DMA((X - 1,)),
            pltpu.SemaphoreType.DMA,
            pltpu.SemaphoreType.DMA((2, X)),
            pltpu.SemaphoreType.DMA((2, X)),
            pltpu.SemaphoreType.DMA((2, 2)),
            pltpu.SemaphoreType.DMA((2, 2)),
        ],
        compiler_params=pltpu.CompilerParams(collective_id=1, has_side_effects=True),
        name="slots_spread",
    )(chosen)


def add_rows(target, terms):
    rows = target.shape[0]

    def step(i, carry):
        at = pl.ds(pl.multiple_of(i * 16, 16), 16)
        total = terms[0][at, :].astype(F32)
        for term in terms[1:]:
            total = total + term[at, :].astype(F32)
        target[at, :] = total.astype(BF16)
        return carry

    lax.fori_loop(0, rows // 16, step, 0)


def collect_kernel(
    part, out, passing, sums, final, stage,
    h_send, h_recv, d_send, d_recv, s_send, s_recv, x_send, x_recv,
):
    x, y, z, c = coords()
    x_peer = [device((x + d) % X, y, z, c) for d in range(X)]
    y_right, y_left, y_far = (y + 1) % Y, (y + Y - 1) % Y, (y + 2) % Y
    right, left = device(x, y_right, z, c), device(x, y_left, z, c)
    entry_barrier(x_peer[1:] + [right, left])
    halves, directs, added = {}, {}, {}
    for i in range(2):
        for way, peer in ((0, right), (1, left)):
            halves[way, i] = remote(
                part.at[y_far, 2 * i + way], passing.at[way, i],
                h_send.at[way, i], h_recv.at[way, i], peer,
            )
            halves[way, i].start()
    for i in range(2):
        for way, peer, goal in ((0, right, y_right), (1, left, y_left)):
            block = 2 * i + 1 - way
            directs[way, i] = remote(
                part.at[goal, block], final.at[way, block],
                d_send.at[way, i], d_recv.at[way, i], peer,
            )
            directs[way, i].start()
    for i in range(2):
        for way, peer, goal in ((0, right, y_right), (1, left, y_left)):
            block = 2 * i + way
            halves[way, i].wait_recv()
            add_rows(sums.at[way, i], [part.at[goal, block], passing.at[way, i]])
            added[way, i] = remote(
                sums.at[way, i], final.at[way, block], s_send.at[way, i], s_recv.at[way, i], peer
            )
            added[way, i].start()
    for i in range(2):
        for way in range(2):
            directs[way, i].wait_recv()
    for i in range(2):
        for way in range(2):
            added[way, i].wait_recv()
    x_copies = []
    for d in (2, 1, 3, 0):
        goal = (x + d) % X
        terms = [part.at[y, goal], final.at[0, goal], final.at[1, goal]]
        if d:
            add_rows(stage.at[d - 1], terms)
            copy = remote(
                stage.at[d - 1], out.at[x], x_send.at[d - 1], x_recv.at[d - 1], x_peer[d]
            )
            copy.start()
            x_copies.append(copy)
        else:
            add_rows(out.at[x], terms)
    for copy in x_copies:
        copy.wait_recv()
    for copy in [*halves.values(), *directs.values(), *added.values(), *x_copies]:
        copy.wait_send()


def collect(part):
    _, _, rows, width = part.shape
    pair = [pltpu.SemaphoreType.DMA((2, 2))] * 6
    return pl.pallas_call(
        collect_kernel,
        out_shape=jax.ShapeDtypeStruct((X, rows, width), BF16),
        in_specs=vmem(1),
        out_specs=vmem(1)[0],
        scratch_shapes=[
            pltpu.VMEM((2, 2, rows, width), BF16),
            pltpu.VMEM((2, 2, rows, width), BF16),
            pltpu.VMEM((2, X, rows, width), BF16),
            pltpu.VMEM((X - 1, rows, width), BF16),
            *pair,
            pltpu.SemaphoreType.DMA((X - 1,)),
            pltpu.SemaphoreType.DMA((X - 1,)),
        ],
        compiler_params=pltpu.CompilerParams(collective_id=2, has_side_effects=True),
        name="slots_collect",
    )(part)


def finish_kernel(part, base, mixed, from_core, stage, from_z, c_send, c_recv, z_send, z_recv):
    x, y, z, c = coords()
    z_peer = [device(x, y, (z + d) % Z, c) for d in range(Z)]
    partner = device(x, y, z, 1 - c)
    entry_barrier(z_peer[1:] + [partner])
    order = (4, 3, 5, 2, 6, 1, 7, 0)
    crossings = {}
    for d in order:
        goal = (z + d) % Z
        crossings[d] = remote(
            part.at[(1 - c) * Z + goal], from_core.at[d], c_send.at[d], c_recv.at[d], partner
        )
        crossings[d].start()
    z_copies = []
    for d in order[:-1]:
        crossings[d].wait_recv()
        goal = c * Z + (z + d) % Z
        stage[d - 1] = (part[goal].astype(F32) + from_core[d].astype(F32)).astype(BF16)
        copy = remote(stage.at[d - 1], from_z.at[d - 1], z_send.at[d - 1], z_recv.at[d - 1], z_peer[d])
        copy.start()
        z_copies.append(copy)
    crossings[0].wait_recv()
    total = base[...] + part[c * Z + z].astype(F32) + from_core[0].astype(F32)
    for copy in z_copies:
        copy.wait_recv()
    for d in range(Z - 1):
        total = total + from_z[d].astype(F32)
    mixed[...] = total.astype(BF16)
    for copy in list(crossings.values()) + z_copies:
        copy.wait_send()


def finish(part, base):
    _, rows, width = part.shape
    return pl.pallas_call(
        finish_kernel,
        out_shape=jax.ShapeDtypeStruct((rows, width), BF16),
        in_specs=vmem(2),
        out_specs=vmem(1)[0],
        scratch_shapes=[
            pltpu.VMEM((Z, rows, width), BF16),
            pltpu.VMEM((Z - 1, rows, width), BF16),
            pltpu.VMEM((Z - 1, rows, width), BF16),
            pltpu.SemaphoreType.DMA((Z,)),
            pltpu.SemaphoreType.DMA((Z,)),
            pltpu.SemaphoreType.DMA((Z - 1,)),
            pltpu.SemaphoreType.DMA((Z - 1,)),
        ],
        compiler_params=pltpu.CompilerParams(collective_id=3, has_side_effects=True),
        name="tokens_finish",
    )(part, base)


def seg_positions(segment_ids):
    length = segment_ids.shape[0]
    indices = jnp.arange(length, dtype=jnp.int32)
    change = jnp.concatenate([jnp.ones((1,), dtype=bool), segment_ids[1:] != segment_ids[:-1]])
    starts = lax.cummax(jnp.where(change, indices, 0), axis=0)
    return indices - starts


def rotate(values, positions):
    half_dim = values.shape[-1] // 2
    inverse = rope_base ** (-jnp.arange(half_dim, dtype=jnp.float32) / half_dim)
    angles = positions.astype(jnp.float32)[:, None] * inverse[None, :]
    cosine = jnp.cos(angles)[:, None, :]
    sine_col = jnp.sin(angles)[:, None, :]
    first_half = values[..., :half_dim]
    second_half = values[..., half_dim:]
    return jnp.concatenate(
        [
            first_half * cosine - second_half * sine_col,
            second_half * cosine + first_half * sine_col,
        ],
        axis=-1,
    )


def attend_group(queries, keys_values, segment_ids, sink_logits):
    length = queries.shape[0]
    kv_heads = keys_values.shape[1] // (2 * HEAD)
    q_heads = queries.shape[1] // HEAD
    group_size = q_heads // kv_heads
    positions = seg_positions(segment_ids)
    q_rot = rotate(queries.astype(jnp.float32).reshape(length, q_heads, HEAD), positions).astype(
        jnp.bfloat16
    )
    q_rot = q_rot.reshape(length, kv_heads, group_size, HEAD)
    key_part = keys_values.reshape(length, kv_heads, 2, HEAD)
    k_rot = rotate(key_part[:, :, 0].astype(jnp.float32), positions).astype(jnp.bfloat16)
    values = key_part[:, :, 1]
    scores = jnp.einsum(
        "qkgd,skd->kgqs", q_rot, k_rot, preferred_element_type=jnp.float32
    ) * HEAD ** (-0.5)
    indices = jnp.arange(length, dtype=jnp.int32)
    visible = (segment_ids[:, None] == segment_ids[None, :]) & (
        indices[None, :] <= indices[:, None]
    )
    scores = jnp.where(visible, scores, -jnp.inf)
    sink_col = sink_logits.reshape(kv_heads, group_size)[:, :, None]
    highest = jnp.maximum(jnp.max(scores, axis=-1), sink_col)
    expo_terms = jnp.exp(scores - highest[..., None])
    denominator = jnp.sum(expo_terms, axis=-1) + jnp.exp(sink_col - highest)
    probabilities = (expo_terms / denominator[..., None]).astype(jnp.bfloat16)
    attended = jnp.einsum(
        "kgqs,skd->qkgd", probabilities, values, preferred_element_type=jnp.float32
    )
    attended = attended.astype(jnp.bfloat16).reshape(length, q_heads * HEAD)
    cached = jnp.stack([k_rot, values], axis=2).reshape(length, kv_heads * 2 * HEAD)
    return (attended, cached)


def route_meta(route_ids, route_weights):
    rows, width = route_ids.shape
    flat = route_ids.reshape(-1)
    index = jnp.arange(rows * width)
    same = (flat[:, None] == flat[None, :]) & (index[None, :] < index[:, None])
    place = jnp.sum(same.astype(F32), axis=1).reshape(rows, width)
    high = route_weights.astype(BF16)
    low = (route_weights - high.astype(F32)).astype(BF16)
    blank = jnp.zeros((rows, META - 4 * width), BF16)
    return jnp.concatenate(
        [route_ids.astype(BF16), place.astype(BF16), high, low, blank], axis=1
    )


def body(
    queries,
    keys_values,
    segments,
    sink_logits,
    out_weight,
    out_bias,
    residual,
    norm_gain,
    route_ids,
    route_logits,
    gate_weight,
    gate_bias,
    up_weight,
    up_bias,
    down_weight,
    down_bias,
    page_table,
):
    width = residual.shape[1]
    tok_count, top = route_ids.shape
    experts = down_bias.shape[0]
    capacity = max(2, 2 * tok_count * top // experts)
    attended, cached = attend_group(queries, keys_values, segments, sink_logits)
    part = jnp.dot(attended, out_weight, preferred_element_type=F32).astype(BF16)
    route_weights = jax.nn.softmax(route_logits, axis=-1)
    meta = route_meta(route_ids, route_weights)
    toks, hidden = project(part, residual, out_bias[None], norm_gain[None], meta)

    toks = toks.reshape(C * Z * tok_count, width + META)
    info = toks[:, width : width + 4 * top].astype(F32)
    ids, place = info[:, :top].astype(jnp.int32), info[:, top : 2 * top].astype(jnp.int32)
    weights = info[:, 2 * top : 3 * top] + info[:, 3 * top : 4 * top]
    source = jnp.arange(C * Z * tok_count, dtype=jnp.int32)[:, None] // tok_count
    slots = C * Z * capacity
    row = (ids // 8) * slots + source * capacity + place
    row = jnp.where(ids % 8 == lax.axis_index("req") % 8, row, -1)
    match = row[:, :, None] == jnp.arange(X * slots, dtype=jnp.int32)[None, None, :]
    pick = jnp.any(match, axis=1).astype(BF16)
    combine = jnp.sum(jnp.where(match, weights[:, :, None], 0.0), axis=1)
    chosen = lax.dot_general(
        pick, toks[:, :width], (((0,), (0,)), ((), ())), preferred_element_type=F32
    ).astype(BF16)
    flat_rows = spread(chosen.reshape(X, slots, width)).reshape(-1, width)

    gate_act = jnp.dot(flat_rows, gate_weight[0], preferred_element_type=F32) + gate_bias[0].astype(F32)
    up_act = jnp.dot(flat_rows, up_weight[0], preferred_element_type=F32) + up_bias[0].astype(F32)
    gate_act = jnp.minimum(gate_act, swiglu_limit)
    up_act = jnp.clip(up_act, -swiglu_limit, swiglu_limit)
    active = (gate_act * jax.nn.sigmoid(glu_alpha * gate_act) * (up_act + 1.0)).astype(BF16)
    partial_value = jnp.dot(active, down_weight[0], preferred_element_type=F32).astype(BF16)

    returned = collect(partial_value.reshape(Y, X, slots, width)).reshape(X * slots, width)
    high = combine.astype(BF16)
    low = (combine - high.astype(F32)).astype(BF16)
    mix = jnp.dot(high, returned, preferred_element_type=F32) + jnp.dot(
        low, returned, preferred_element_type=F32
    )
    expert_onehot = (
        route_ids[:, :, None] == jnp.arange(experts, dtype=jnp.int32)[None, None, :]
    ).astype(F32)
    dense_weights = jnp.einsum(
        "rk,rke->re", route_weights, expert_onehot, precision=lax.Precision.HIGHEST
    )
    base = hidden.astype(F32) + jnp.dot(
        dense_weights,
        down_bias.astype(F32),
        precision=lax.Precision.HIGHEST,
        preferred_element_type=F32,
    )
    mixed_out = finish(mix.astype(BF16).reshape(C * Z, tok_count, width), base)
    blocks = cached.reshape(-1, PAGE_LEN, cached.shape[1])
    page_pool = jnp.zeros_like(blocks).at[page_table[0]].set(blocks)
    return (mixed_out, page_pool)


def solution(mesh):
    in_specs = (
        P("req", "tp"),
        P("req", "tp"),
        P("req"),
        P("tp"),
        P("tp", None),
        P(),
        P(("req", "tp"), None),
        P(),
        P(("req", "tp"), None),
        P(("req", "tp"), None),
        P("req", None, "tp"),
        P("req", "tp"),
        P("req", None, "tp"),
        P("req", "tp"),
        P("req", "tp", None),
        P(),
        P("req", None),
    )
    out_specs = (P(("req", "tp"), None), P("req", None, "tp"))
    return jax.shard_map(body, mesh=mesh, in_specs=in_specs, out_specs=out_specs, check_vma=False)
```

time: 544 us -> 270 us (0.50)
  waiting for transfers between devices: 341 us -> 0 us
  Pallas kernels: 0 us -> 215 us
  blocking collectives: 83.5 us -> 0 us
  local copies, waits for them, and re-layouts: 55 us -> 23 us
  starting transfers between devices: 21.3 us -> 0 us
  between operations: 14.5 us -> 1.08 us
    pallas_call x0 -> x4, Pallas kernels: none -> 215 us  [the longest x1 73.8 us: collect(): pl.pallas_call(collect_kernel, out_shape=jax.ShapeDtypeStruct((X, rows, w...]
    reduce_scatter x2 -> x0, waiting for transfers between devices: 188 us -> none  [the longest x1 147 us: body(): lax.psum_scatter(partial_value.astype(jnp.bfloat16), 'tp', scatter_dimens...]
    all_to_all x2 -> x0, waiting for transfers between devices: 153 us -> none  [the longest x1 134 us: body(): lax.all_to_all(dispatched, 'req', split_axis=0, concat_axis=0, tiled=True)]
    all_gather x2 -> x0, blocking collectives: 83.5 us -> none  [the longest x1 46 us: body(): lax.all_gather(normed, 'tp', axis=0, tiled=True)]
    reshape x4 -> x0, local copies, waits for them, and re-layouts: 23.3 us -> none  [the longest x1 10.7 us: body(): dispatch(group_rows, all_slots, experts * tp_count * capacity)]
    all_to_all x2 -> x0, starting transfers between devices: 21 us -> none  [the longest x1 14.4 us: body(): lax.all_to_all(dispatched, 'req', split_axis=0, concat_axis=0, tiled=True)]
    gather x1 -> x0, local copies, waits for them, and re-layouts: 12.9 us -> none  [dispatch(): return padded[member]]
    convert_element_type x2 -> x6, local copies, waits for them, and re-layouts: 6.63 us -> 16.2 us  [the longest x1 8.5 us: body(): jnp.dot(active, down_weight[0], preferred_element_type=F32).astype(BF16)]
  transfers between devices with their start and end apart: 4 -> 0, of which waited for: 4 -> 0; matrix products, arithmetic and copies ran while one was open for 1% -> 0% of each run, Pallas kernels for 0% -> 0%
where the time goes in v1:
time: 270 us; the launch traced here: 269 us
  Pallas kernels  215 us (80%)
  matrix products  24.9 us (9%)
  local copies, waits for them, and re-layouts  23 us (9%)
  other arithmetic  4.96 us (2%)
    pallas_call x1, Pallas kernels, collect(): pl.pallas_call(collect_kernel, out_shape=jax.ShapeDtypeStruct((X, rows, w...  73.8 us
    pallas_call x1, Pallas kernels, spread(): pl.pallas_call(spread_kernel, out_shape=jax.ShapeDtypeStruct((Y, X, rows,...  67.5 us
    pallas_call x1, Pallas kernels, project(): pl.pallas_call(project_kernel, out_shape=(jax.ShapeDtypeStruct((C * Z, ro...  48.8 us
    pallas_call x1, Pallas kernels, finish(): pl.pallas_call(finish_kernel, out_shape=jax.ShapeDtypeStruct((rows, width...  25.3 us
    convert_element_type x1, local copies, waits for them, and re-layouts, body(): jnp.dot(active, down_weight[0], preferred_element_type=F32).astype(BF16)  8.5 us
    dot_general x1, matrix products, body(): jnp.dot(flat_rows, up_weight[0], preferred_element_type=F32)  5.98 us

profile of v1, /device:TPU:1, one launch (start us, length us, event | category | flops | bytes accessed | tf_op | source)
XLA Modules:
  0.0 269.3 jit_solution(7814115714598015324)
XLA Ops:
  0.7 0.9 compare_bitcast_fusion
  1.6 0.1 copy.61
  1.8 0.2 reduce-window.8
  1.9 0.1 reduce.2
  2.1 0.1 multiply_cosine_fusion
  2.2 1.0 copy.62
  3.3 0.9 copy.60
  4.2 0.1 fusion.35
  4.3 0.8 fusion.27
  5.1 0.3 fusion.51
  5.5 0.1 fusion.12
  5.6 0.2 convolution_convert_fusion.3
  5.9 1.8 convolution_convert_fusion.2
  7.7 2.3 copy.67.part
  10.0 0.1 copy.65
  10.1 0.2 fusion.44
  10.4 0.1 copy.64
  10.5 0.1 eq.67
  10.6 0.2 convert_reduce_fusion
  10.8 0.1 convert_element_type.128
  10.9 0.1 copy.66
  11.0 0.7 concatenate.52.meta
  11.7 0.6 broadcast_in_dim.33.bias
  12.3 0.6 broadcast_in_dim.34.gain
  12.9 48.8 %project_gather.1 = (bf16[16,16,2944]{2,1,0:T(8,128)(2,1)}, bf16[16,2880]{1,0:T(8,128)(2,1)}) custom-call(bf16[128,2880]{1,0:T(8,128)(2,1)} %copy.67.part, bf16[16,2880]{1,0:T(8,128)(2,1)} %residual.1, bf16[1,2880]{1,0:T(2,128)(2,1)} %broadcast_in_dim.33.bias, bf16[1,2880]{1,0:T(2,128)(2,1)} %broadcast_in_dim.34.gain, bf16[16,64]{1,0:T(8,128)(2,1)} %concatenate.52.meta), custom_call_target="tpu_custom_call" | custom-call | tf_op jit(solution)/shard_map/project_gather/pallas_call | solution.py:111
  61.7 0.9 slice_convert_fusion.2
  62.6 0.2 fusion.18
  62.9 0.2 fusion.11
  63.1 3.2 %convolution_convert_fusion.1 = bf16[256,2880]{0,1:T(8,128)(2,1)} fusion(pred[256,256]{1,0:T(8,128)(4,1)S(1)} %fusion.11, bf16[256,2944]{1,0:T(8,128)(2,1)} %bitcast.86), kind=kOutput, calls=%fused_computation.4 | convolution fusion | flops 378224640 | bytes 3047424 | tf_op jit(solution)/shard_map/dot_general | solution.py:459
  66.3 2.5 copy.70
  68.9 67.5 %slots_spread.1 = bf16[4,4,64,2880]{3,2,1,0:T(8,128)(2,1)} custom-call(bf16[4,64,2880]{2,1,0:T(8,128)(2,1)} %bitcast.81), custom_call_target="tpu_custom_call" | custom-call | tf_op jit(solution)/shard_map/slots_spread/pallas_call | solution.py:179
  136.4 6.0 %fusion.2 = f32[1024,360]{0,1:T(8,128)S(1)} fusion(bf16[1024,2880]{1,0:T(8,128)(2,1)} %bitcast.82, bf16[1,2880,360]{1,2,0:T(8,128)(2,1)} %param.29), kind=kOutput, calls=%fused_computation.8 | convolution fusion | flops 2123366400 | bytes 9446400 | tf_op jit(solution)/shard_map/dot_general | solution.py:465
  142.5 2.9 %multiply_convert_fusion = bf16[1024,360]{0,1:T(8,128)(2,1)S(1)} fusion(f32[1024,360]{0,1:T(8,128)S(1)} %fusion.2, bf16[1024,2880]{1,0:T(8,128)(2,1)S(1)} %bitcast.83, bf16[1,2880,360]{1,2,0:T(8,128)(2,1)S(1)} %copy-done.13, f32[360]{0:T(512)S(1)} %get-tuple-element.19, f32[360]{0:T(512)S(1)} %get-tuple-element.20), kind=kOutput, calls=%fused_computation.13 | convolution fusion | flops 2127790080 | bytes 10186560 | tf_op jit(solution)/shard_map/dot_general | solution.py:464
  145.4 5.2 %convolution_convert_fusion = bf16[1024,2880]{0,1:T(8,128)(2,1)} fusion(bf16[1024,360]{0,1:T(8,128)(2,1)S(1)} %multiply_convert_fusion, bf16[1,360,2880]{2,1,0:T(8,128)(2,1)S(1)} %copy-done.14), kind=kOutput, calls=%fused_computation.1 | convolution fusion | flops 2126315520 | bytes 8709120 | tf_op jit(solution)/shard_map/dot_general | solution.py:469
  150.7 8.5 %copy.71 = bf16[1024,2880]{1,0:T(8,128)(2,1)} copy(bf16[1024,2880]{0,1:T(8,128)(2,1)} %convolution_convert_fusion) | data formatting | bytes 11796480 | tf_op jit(solution)/shard_map/convert_element_type | solution.py:469
  159.2 73.8 %slots_collect.1 = bf16[4,64,2880]{2,1,0:T(8,128)(2,1)} custom-call(bf16[4,4,64,2880]{3,2,1,0:T(8,128)(2,1)} %bitcast.78), custom_call_target="tpu_custom_call" | custom-call | tf_op jit(solution)/shard_map/slots_collect/pallas_call | solution.py:274
  233.0 0.1 slice_add_fusion
  233.2 0.4 select_reduce_fusion
  233.5 2.2 fusion.25
  235.8 1.9 fusion
  237.7 2.6 copy.72
  240.3 0.3 fusion.29
  240.6 0.9 convolution_add_fusion.1.base
  241.4 25.3 %tokens_finish.1 = bf16[16,2880]{1,0:T(8,128)(2,1)} custom-call(bf16[16,16,2880]{2,1,0:T(8,128)(2,1)} %bitcast.84, f32[16,2880]{1,0:T(8,128)} %convolution_add_fusion.1.base), custom_call_target="tpu_custom_call" | custom-call | tf_op jit(solution)/shard_map/tokens_finish/pallas_call | solution.py:327
  266.8 0.1 copy.74
  266.9 0.1 reshape.430
  267.0 0.7 scatter_fusion
  267.8 1.5 copy.80
  (50 shorter events, 0.7 us)
Async XLA Ops:
  0.6 5.3 %copy-start = (bf16[512,2880]{0,1:T(8,128)(2,1)S(1)}, bf16[512,2880]{0,1:T(8,128)(2,1)}, u32[]{:S(2)}) copy-start(bf16[512,2880]{0,1:T(8,128)(2,1)} %param.21) | copy-start | bytes 8847364
  0.6 4.8 %copy-start.10 = (f32[8]{0:T(128)S(1)}, f32[8]{0:T(128)}, u32[]{:S(2)}) copy-start(f32[8]{0:T(128)} %param.20) | copy-start | bytes 100
  5.9 4.1 %copy-start.6 = (f32[16,4]{0,1:T(4,128)S(1)}, f32[16,4]{0,1:T(4,128)}, u32[]{:S(2)}) copy-start(f32[16,4]{0,1:T(4,128)} %param.26) | copy-start | bytes 772
  7.7 2.7 copy-start.7
  7.7 4.0 %copy-start.8 = (bf16[2880]{0:T(1024)(128)(2,1)S(1)}, bf16[2880]{0:T(1024)(128)(2,1)}, u32[]{:S(2)}) copy-start(bf16[2880]{0:T(1024)(128)(2,1)} %param.22) | copy-start | bytes 17284
  7.7 4.6 %copy-start.9 = (bf16[2880]{0:T(1024)(128)(2,1)S(1)}, bf16[2880]{0:T(1024)(128)(2,1)}, u32[]{:S(2)}) copy-start(bf16[2880]{0:T(1024)(128)(2,1)} %param.24) | copy-start | bytes 17284
  136.4 6.0 %copy-start.11 = (bf16[1,360]{1,0:T(2,128)(2,1)S(1)}, bf16[1,360]{1,0:T(2,128)(2,1)}, u32[]{:S(2)}) copy-start(bf16[1,360]{1,0:T(2,128)(2,1)} %param.30) | copy-start | bytes 2164
  136.4 6.0 %copy-start.12 = (bf16[1,360]{1,0:T(2,128)(2,1)S(1)}, bf16[1,360]{1,0:T(2,128)(2,1)}, u32[]{:S(2)}) copy-start(bf16[1,360]{1,0:T(2,128)(2,1)} %param.28) | copy-start | bytes 2164
  136.4 6.1 %copy-start.2 = (bf16[4,4,64,2880]{3,2,1,0:T(8,128)(2,1)S(1)}, bf16[4,4,64,2880]{3,2,1,0:T(8,128)(2,1)}, u32[]{:S(2)}) copy-start(bf16[4,4,64,2880]{3,2,1,0:T(8,128)(2,1)} %slots_spread.1) | copy-start | bytes 17694724
  136.4 6.1 %copy-start.13 = (bf16[1,2880,360]{1,2,0:T(8,128)(2,1)S(1)}, bf16[1,2880,360]{1,2,0:T(8,128)(2,1)}, u32[]{:S(2)}) copy-start(bf16[1,2880,360]{1,2,0:T(8,128)(2,1)} %param.27) | copy-start | bytes 6220804
  142.5 2.9 %copy-start.14 = (bf16[1,360,2880]{2,1,0:T(8,128)(2,1)S(1)}, bf16[1,360,2880]{2,1,0:T(8,128)(2,1)}, u32[]{:S(2)}) copy-start(bf16[1,360,2880]{2,1,0:T(8,128)(2,1)} %param.31) | copy-start | bytes 6220804
  233.5 2.3 copy-start.1
  237.7 2.9 %copy-start.3 = (bf16[32,2880]{1,0:T(8,128)(2,1)S(1)}, bf16[32,2880]{1,0:T(8,128)(2,1)}, u32[]{:S(2)}) copy-start(bf16[32,2880]{1,0:T(8,128)(2,1)} %param.32) | copy-start | bytes 552964
  237.7 2.9 %copy-start.5 = (bf16[16,2880]{1,0:T(8,128)(2,1)S(1)}, bf16[16,2880]{1,0:T(8,128)(2,1)}, u32[]{:S(2)}) copy-start(bf16[16,2880]{1,0:T(8,128)(2,1)} %get-tuple-element.5) | copy-start | bytes 276484
  240.3 26.7 %copy-start.15 = (s32[1,8]{1,0:T(1,128)S(1)}, s32[1,8]{1,0:T(1,128)}, u32[]{:S(2)}) copy-start(s32[1,8]{1,0:T(1,128)} %param.33) | copy-start | bytes 100
  267.8 1.6 copy-start.4
